TPU v7x, 32 devices: a whole 2x2x4 slice. The times are simulated.
32 devices in a mesh: dp: 16 (over z, y, core), query: 2 (over x).
Axes of the slice: x: 2, y: 2, z: 4, core: 2. Of those that a mesh axis runs over, the one named last changes fastest.
Arguments:
- tokens: bfloat16 [2, 32, 128, 1280], P(None, ('dp', 'query')), may hold values from -6 to 6
- out_cotangent: bfloat16 [2, 32, 128, 1280], P(None, ('dp', 'query')), may hold values from -6 to 6
- qkv_weight: bfloat16 [1280, 3840], P('dp'), may hold values from -0.15625 to 0.15625
- out_weight: bfloat16 [1280, 1280], P('dp'), may hold values from -0.625 to 0.625
- up_weight: bfloat16 [1280, 5120], P('dp'), may hold values from -0.15625 to 0.15625
- down_weight: bfloat16 [5120, 1280], P('dp'), may hold values from -0.078125 to 0.078125
- attn_gain: bfloat16 [1280], P('dp'), may hold values from 0.5 to 1.5
- ffn_gain: bfloat16 [1280], P('dp'), may hold values from 0.5 to 1.5
- up_bias: bfloat16 [5120], P('dp'), may hold values from -3 to 3
- cell_weight: bfloat16 [1280, 5120], P('dp'), may hold values from -0.15625 to 0.15625
- gene_weight: bfloat16 [1280, 5120], P('dp'), may hold values from -0.15625 to 0.15625
- decoder_bias: bfloat16 [5120], P('dp'), may hold values from -3 to 3
- readout: bfloat16 [5120], P('dp'), may hold values from -0.15625 to 0.15625
- gene_embed: bfloat16 [2, 32, 384, 1280], P(None, ('dp', 'query')), may hold values from -6 to 6
- query_cell: int32 [2, 32, 384], P(None, ('dp', 'query')), may hold values from 0 to 1
- query_label: int32 [2, 32, 384], P(None, ('dp', 'query')), may hold values 0 or 1
- query_live: int32 [16, 2, 2], P('dp', None, 'query'), may hold values from 1 to 384, 480 in all within a row
Outputs:
- block_out: bfloat16 [2, 32, 128, 1280], P(None, ('dp', 'query'))
- grad_tokens: float32 [2, 32, 128, 1280], P(None, ('dp', 'query'))
- grad_qkv: float32 [1280, 3840], P('dp')
- grad_out: float32 [1280, 1280], P('dp')
- grad_up: float32 [1280, 5120], P('dp')
- grad_down: float32 [5120, 1280], P('dp')
- grad_attn_gain: float32 [1280], P('dp')
- grad_ffn_gain: float32 [1280], P('dp')
- grad_up_bias: float32 [5120], P('dp')
- grad_cell: float32 [1280, 5120], P('dp')
- grad_gene: float32 [1280, 5120], P('dp')
- grad_decoder_bias: float32 [5120], P('dp')
- grad_readout: float32 [5120], P('dp')
Inputs may be any that keep to these rules, and one draw needn't show every extreme that they name: `query_live`: the 2 devices of one dp index together hold 480 live rows in each micro-batch; a device's live rows are its first slots. `query_cell`: index of a cell within the query group of the row's device.
All inputs are finite; a program needn't handle non-finite values. No bound on the sum of `query_label` on one device may be relied on, other than what follows from the above.
Results may differ from a plain program's by a relative error of at most 0.02.
Values may be sent and summed in bfloat16 or wider, within the bound.
No kernel may reach another device: no remote copies, remote signals or barrier semaphores. Data moves between devices by JAX's collectives and lax.ppermute only.
A program may use at most 320 MiB of HBM per device.

v0:
```python
import jax
import jax.numpy as jnp
from jax import lax
from jax.sharding import PartitionSpec as P

D = 1280
HEADS = 20
HEAD = 64
highest = lax.Precision.HIGHEST
epsilon = 1e-05


def row_product(left, right):
    return lax.dot_general(
        left, right, (((0,), (0,)), ((), ())), preferred_element_type=jnp.float32
    )


def times_transpose(left, right):
    return lax.dot_general(
        left, right, (((1,), (1,)), ((), ())), preferred_element_type=jnp.float32
    )


def layer_stats(values):
    average = jnp.mean(values, axis=-1, keepdims=True)
    centred = values - average
    variance = jnp.mean(centred * centred, axis=-1, keepdims=True)
    inverse = lax.rsqrt(variance + epsilon)
    return (centred * inverse, inverse)


def norm_back(grad_scaled, gain, normal, inverse):
    grad_normal = grad_scaled * gain
    along_normal = jnp.mean(grad_normal * normal, axis=-1, keepdims=True)
    average = jnp.mean(grad_normal, axis=-1, keepdims=True)
    grad_values = inverse * (grad_normal - average - normal * along_normal)
    return (grad_values, jnp.sum(grad_scaled * normal, axis=0))


def encode(inputs, weights):
    qkv_weight, out_weight, up_weight, down_weight, attn_gain, ffn_gain, up_bias = weights
    length = inputs.shape[0]
    tokens_wide = inputs.astype(jnp.float32)
    norm_one, scale_one = layer_stats(tokens_wide)
    normed = (norm_one * attn_gain.astype(jnp.float32)).astype(jnp.bfloat16)
    projected = jnp.dot(normed, qkv_weight, preferred_element_type=jnp.float32).astype(jnp.bfloat16)
    projected = projected.reshape(length, 3, HEADS, HEAD)
    queries = projected[:, 0]
    key_heads = projected[:, 1]
    value_heads = projected[:, 2]
    scores = (
        jnp.einsum("qhd,khd->hqk", queries, key_heads, preferred_element_type=jnp.float32) * 0.125
    )
    row_max = jnp.max(scores, axis=-1, keepdims=True)
    shifted = jnp.exp(scores - row_max)
    row_total = jnp.sum(shifted, axis=-1, keepdims=True)
    attn_probs = (shifted / row_total).astype(jnp.bfloat16)
    logsum = row_max + jnp.log(row_total)
    mixed_heads = jnp.einsum(
        "hqk,khd->qhd", attn_probs, value_heads, preferred_element_type=jnp.float32
    )
    mixed_heads = mixed_heads.astype(jnp.bfloat16).reshape(length, D)
    hidden = tokens_wide + jnp.dot(mixed_heads, out_weight, preferred_element_type=jnp.float32)
    norm_two, scale_two = layer_stats(hidden)
    second = (norm_two * ffn_gain.astype(jnp.float32)).astype(jnp.bfloat16)
    up_proj = jnp.dot(second, up_weight, preferred_element_type=jnp.float32) + up_bias.astype(
        jnp.float32
    )
    active = jax.nn.gelu(up_proj, approximate=True).astype(jnp.bfloat16)
    output = hidden + jnp.dot(active, down_weight, preferred_element_type=jnp.float32)
    saved_state = (
        norm_one,
        scale_one,
        normed,
        queries,
        key_heads,
        value_heads,
        logsum,
        mixed_heads,
        norm_two,
        scale_two,
        second,
        up_proj,
        active,
    )
    return (output, saved_state)


def encode_back(grad_output, saved_state, weights):
    qkv_weight, out_weight, up_weight, down_weight, attn_gain, ffn_gain = weights
    (
        norm_one,
        scale_one,
        normed,
        queries,
        key_heads,
        value_heads,
        logsum,
        mixed_heads,
        norm_two,
        scale_two,
        second,
        up_proj,
        active,
    ) = saved_state
    length = grad_output.shape[0]
    grad_branch = grad_output.astype(jnp.bfloat16)
    grad_down = row_product(active, grad_branch)
    grad_active = times_transpose(grad_branch, down_weight)
    gelu_back = jax.vjp(lambda inner_values: jax.nn.gelu(inner_values, approximate=True), up_proj)[
        1
    ]
    grad_up_proj = gelu_back(grad_active)[0].astype(jnp.bfloat16)
    grad_up = row_product(second, grad_up_proj)
    grad_up_bias = jnp.sum(grad_up_proj.astype(jnp.float32), axis=0)
    grad_second = times_transpose(grad_up_proj, up_weight)
    grad_hidden_norm, grad_ffn_gain = norm_back(
        grad_second, ffn_gain.astype(jnp.float32), norm_two, scale_two
    )
    grad_hidden = grad_output + grad_hidden_norm
    grad_attn = grad_hidden.astype(jnp.bfloat16)
    grad_out = row_product(mixed_heads, grad_attn)
    grad_mixed = (
        times_transpose(grad_attn, out_weight).astype(jnp.bfloat16).reshape(length, HEADS, HEAD)
    )
    scores = (
        jnp.einsum("qhd,khd->hqk", queries, key_heads, preferred_element_type=jnp.float32) * 0.125
    )
    attn_probs = jnp.exp(scores - logsum)
    probs_low = attn_probs.astype(jnp.bfloat16)
    grad_values = jnp.einsum(
        "hqk,qhd->khd", probs_low, grad_mixed, preferred_element_type=jnp.float32
    )
    grad_probs = jnp.einsum(
        "qhd,khd->hqk", grad_mixed, value_heads, preferred_element_type=jnp.float32
    )
    along_probs = jnp.sum(grad_probs * attn_probs, axis=-1, keepdims=True)
    grad_scores = (attn_probs * (grad_probs - along_probs) * 0.125).astype(jnp.bfloat16)
    grad_queries = jnp.einsum(
        "hqk,khd->qhd", grad_scores, key_heads, preferred_element_type=jnp.float32
    )
    grad_keys = jnp.einsum("hqk,qhd->khd", grad_scores, queries, preferred_element_type=jnp.float32)
    grad_projected = (
        jnp.stack([grad_queries, grad_keys, grad_values], axis=1)
        .astype(jnp.bfloat16)
        .reshape(length, 3 * D)
    )
    grad_qkv = row_product(normed, grad_projected)
    grad_normed = times_transpose(grad_projected, qkv_weight)
    grad_input_norm, grad_attn_gain = norm_back(
        grad_normed, attn_gain.astype(jnp.float32), norm_one, scale_one
    )
    grad_input = grad_hidden + grad_input_norm
    return (
        (grad_qkv, grad_out, grad_up, grad_down, grad_attn_gain, grad_ffn_gain, grad_up_bias),
        grad_input,
    )


def decode(summary_all, weights, gene_rows, cell_ids, labels, live_count):
    cell_weight, gene_weight, decoder_bias, readout = weights
    group_size = summary_all.shape[0]
    slot_count = gene_rows.shape[0]
    cell_part = jnp.dot(summary_all, cell_weight, preferred_element_type=jnp.float32)
    onehot = (cell_ids[:, None] == jnp.arange(group_size, dtype=jnp.int32)[None, :]).astype(
        jnp.float32
    )
    picked = jnp.dot(onehot, cell_part, precision=highest)
    pre_act = (
        picked
        + jnp.dot(gene_rows, gene_weight, preferred_element_type=jnp.float32)
        + decoder_bias.astype(jnp.float32)
    )
    activity, silu_back = jax.vjp(jax.nn.silu, pre_act)
    read_wide = readout.astype(jnp.float32)
    logits = jnp.sum(activity * read_wide[None, :], axis=-1)
    live_rows = (jnp.arange(slot_count, dtype=jnp.int32) < live_count).astype(jnp.float32)
    grad_logits = live_rows * (jax.nn.sigmoid(logits) - labels.astype(jnp.float32))
    grad_readout = jnp.sum(grad_logits[:, None] * activity, axis=0)
    grad_pre = silu_back(grad_logits[:, None] * read_wide[None, :])[0].astype(jnp.bfloat16)
    grad_pre_wide = grad_pre.astype(jnp.float32)
    grad_decoder_bias = jnp.sum(grad_pre_wide, axis=0)
    grad_gene = row_product(gene_rows, grad_pre)
    grad_cellproj = lax.dot_general(
        onehot, grad_pre_wide, (((0,), (0,)), ((), ())), precision=highest
    )
    grad_cell = lax.dot_general(
        summary_all.astype(jnp.float32), grad_cellproj, (((0,), (0,)), ((), ())), precision=highest
    )
    grad_summary = lax.dot_general(
        grad_cellproj, cell_weight.astype(jnp.float32), (((1,), (1,)), ((), ())), precision=highest
    )
    return ((grad_cell, grad_gene, grad_decoder_bias, grad_readout), grad_summary)


def shards(
    tokens,
    out_cotangent,
    qkv_weight,
    out_weight,
    up_weight,
    down_weight,
    attn_gain,
    ffn_gain,
    up_bias,
    cell_weight,
    gene_weight,
    decoder_bias,
    readout,
    gene_embed,
    query_cell,
    query_label,
    query_live,
):
    micro_count = tokens.shape[0]
    outputs = []
    input_grads = []
    totals = None
    for micro_index in range(micro_count):
        gathered = (
            lax.all_gather(qkv_weight, "dp", axis=0, tiled=True),
            lax.all_gather(out_weight, "dp", axis=0, tiled=True),
            lax.all_gather(up_weight, "dp", axis=0, tiled=True),
            lax.all_gather(down_weight, "dp", axis=0, tiled=True),
            lax.all_gather(attn_gain, "dp", axis=0, tiled=True),
            lax.all_gather(ffn_gain, "dp", axis=0, tiled=True),
            lax.all_gather(up_bias, "dp", axis=0, tiled=True),
            lax.all_gather(cell_weight, "dp", axis=0, tiled=True),
            lax.all_gather(gene_weight, "dp", axis=0, tiled=True),
            lax.all_gather(decoder_bias, "dp", axis=0, tiled=True),
            lax.all_gather(readout, "dp", axis=0, tiled=True),
        )
        output, saved_state = encode(tokens[micro_index, 0], gathered[:7])
        outputs.append(output.astype(jnp.bfloat16))
        summary_all = lax.all_gather(output[0:1].astype(jnp.bfloat16), "query", axis=0, tiled=True)
        decoder_grads, grad_summary = decode(
            summary_all,
            gathered[7:],
            gene_embed[micro_index, 0],
            query_cell[micro_index, 0],
            query_label[micro_index, 0],
            query_live[0, micro_index, 0],
        )
        grad_own = lax.psum_scatter(
            grad_summary.astype(jnp.bfloat16), "query", scatter_dimension=0, tiled=True
        ).astype(jnp.float32)
        grad_output = out_cotangent[micro_index, 0].astype(jnp.float32)
        grad_output = grad_output.at[0:1].add(grad_own)
        back_weights = (
            lax.all_gather(qkv_weight, "dp", axis=0, tiled=True),
            lax.all_gather(out_weight, "dp", axis=0, tiled=True),
            lax.all_gather(up_weight, "dp", axis=0, tiled=True),
            lax.all_gather(down_weight, "dp", axis=0, tiled=True),
            lax.all_gather(attn_gain, "dp", axis=0, tiled=True),
            lax.all_gather(ffn_gain, "dp", axis=0, tiled=True),
        )
        encoder_grads, grad_input = encode_back(grad_output, saved_state, back_weights)
        input_grads.append(grad_input)
        step_grads = encoder_grads + decoder_grads
        if micro_index == 0:
            totals = tuple(step_grads)
        else:
            totals = tuple((earlier + later for earlier, later in zip(totals, step_grads)))
    owned = (
        lax.psum_scatter(
            totals[0].astype(jnp.bfloat16), "dp", scatter_dimension=0, tiled=True
        ).astype(jnp.float32),
        lax.psum_scatter(
            totals[1].astype(jnp.bfloat16), "dp", scatter_dimension=0, tiled=True
        ).astype(jnp.float32),
        lax.psum_scatter(
            totals[2].astype(jnp.bfloat16), "dp", scatter_dimension=0, tiled=True
        ).astype(jnp.float32),
        lax.psum_scatter(
            totals[3].astype(jnp.bfloat16), "dp", scatter_dimension=0, tiled=True
        ).astype(jnp.float32),
        lax.psum_scatter(
            totals[4].astype(jnp.bfloat16), "dp", scatter_dimension=0, tiled=True
        ).astype(jnp.float32),
        lax.psum_scatter(
            totals[5].astype(jnp.bfloat16), "dp", scatter_dimension=0, tiled=True
        ).astype(jnp.float32),
        lax.psum_scatter(
            totals[6].astype(jnp.bfloat16), "dp", scatter_dimension=0, tiled=True
        ).astype(jnp.float32),
        lax.psum_scatter(
            totals[7].astype(jnp.bfloat16), "dp", scatter_dimension=0, tiled=True
        ).astype(jnp.float32),
        lax.psum_scatter(
            totals[8].astype(jnp.bfloat16), "dp", scatter_dimension=0, tiled=True
        ).astype(jnp.float32),
        lax.psum_scatter(
            totals[9].astype(jnp.bfloat16), "dp", scatter_dimension=0, tiled=True
        ).astype(jnp.float32),
        lax.psum_scatter(
            totals[10].astype(jnp.bfloat16), "dp", scatter_dimension=0, tiled=True
        ).astype(jnp.float32),
    )
    totals = (
        lax.psum(owned[0].astype(jnp.bfloat16), "query").astype(jnp.float32),
        lax.psum(owned[1].astype(jnp.bfloat16), "query").astype(jnp.float32),
        lax.psum(owned[2].astype(jnp.bfloat16), "query").astype(jnp.float32),
        lax.psum(owned[3].astype(jnp.bfloat16), "query").astype(jnp.float32),
        lax.psum(owned[4].astype(jnp.bfloat16), "query").astype(jnp.float32),
        lax.psum(owned[5].astype(jnp.bfloat16), "query").astype(jnp.float32),
        lax.psum(owned[6].astype(jnp.bfloat16), "query").astype(jnp.float32),
        lax.psum(owned[7].astype(jnp.bfloat16), "query").astype(jnp.float32),
        lax.psum(owned[8].astype(jnp.bfloat16), "query").astype(jnp.float32),
        lax.psum(owned[9].astype(jnp.bfloat16), "query").astype(jnp.float32),
        lax.psum(owned[10].astype(jnp.bfloat16), "query").astype(jnp.float32),
    )
    block_out = jnp.stack(outputs, axis=0)[:, None]
    grad_tokens = jnp.stack(input_grads, axis=0)[:, None]
    return (
        block_out,
        grad_tokens,
        totals[0],
        totals[1],
        totals[2],
        totals[3],
        totals[4],
        totals[5],
        totals[6],
        totals[7],
        totals[8],
        totals[9],
        totals[10],
    )


def solution(mesh):
    placed = (
        P(None, ("dp", "query"), None, None),
        P(None, ("dp", "query"), None, None),
        P("dp", None),
        P("dp", None),
        P("dp", None),
        P("dp", None),
        P("dp"),
        P("dp"),
        P("dp"),
        P("dp", None),
        P("dp", None),
        P("dp"),
        P("dp"),
        P(None, ("dp", "query"), None, None),
        P(None, ("dp", "query"), None),
        P(None, ("dp", "query"), None),
        P("dp", None, "query"),
    )
    return jax.shard_map(
        shards,
        mesh=mesh,
        in_specs=placed,
        out_specs=(
            P(None, ("dp", "query"), None, None),
            P(None, ("dp", "query"), None, None),
            P("dp", None),
            P("dp", None),
            P("dp", None),
            P("dp", None),
            P("dp"),
            P("dp"),
            P("dp"),
            P("dp", None),
            P("dp", None),
            P("dp"),
            P("dp"),
        ),
        check_vma=False,
    )
```

profile of v0, /device:TPU:0, one launch (start us, length us, event | category | flops | bytes accessed | tf_op | source)
XLA Modules:
  0.0 1549.0 jit_solution(1948422574728645002)
XLA Ops:
  14.5 65.3 %all-reduce.13 = (bf16[1280]{0:T(1024)(128)(2,1)S(1)}, bf16[5120]{0:T(1024)(128)(2,1)S(1)}, bf16[1280]{0:T(1024)(128)(2,1)S(1)}, bf16[5120]{0:T(1024)(128)(2,1)S(1)}, bf16[5120]{0:T(1024)(128)(2,1)S(1)}) all-reduce(bf16[1280]{0:T(1024)(128)(2,1)S(1)} %dynamic-update-slice.6, ...), channel_id=1, replica_groups=mesh['dp'=16,'query'=2] {'dp'}, use_global_device_ids=true, to_apply=%add | all-reduce | flops 17920 | bytes 71680
  81.0 16.6 %all-gather.9.cloned.1.call-done = bf16[1280,3840]{1,0:T(8,128)(2,1)} async-done(((bf16[80,3840]{1,0:T(8,128)(2,1)}), bf16[1280,3840]{1,0:T(8,128)(2,1)}) %all-gather.9.cloned.1.call-update) | async-done | bytes 9830416 | tf_op jit(solution)/shard_map/all_gather | solution.py:222
  97.6 5.3 convolution_convert_fusion
  103.7 5.9 convolution_convert_fusion.1
  112.9 31.2 %all-gather.11.cloned.1.call-done = bf16[1280,1280]{1,0:T(8,128)(2,1)} async-done(((bf16[80,1280]{1,0:T(8,128)(2,1)}), bf16[1280,1280]{1,0:T(8,128)(2,1)}) %all-gather.11.cloned.1.call-update) | async-done | bytes 3276816 | tf_op jit(solution)/shard_map/all_gather | solution.py:223
  144.1 2.7 fusion.191
  151.0 98.3 %all-gather.13.cloned.1.call-done = bf16[1280,5120]{1,0:T(8,128)(2,1)} async-done(((bf16[80,5120]{1,0:T(8,128)(2,1)}), bf16[1280,5120]{1,0:T(8,128)(2,1)}) %all-gather.13.cloned.1.call-update) | async-done | bytes 13107216 | tf_op jit(solution)/shard_map/all_gather | solution.py:224
  249.3 8.2 convolution_add_fusion.1
  257.5 96.1 %all-gather.15.cloned.1.call-done = bf16[5120,1280]{1,0:T(8,128)(2,1)} async-done(((bf16[320,1280]{1,0:T(8,128)(2,1)}), bf16[5120,1280]{1,0:T(8,128)(2,1)}) %all-gather.15.cloned.1.call-update) | async-done | bytes 13107216 | tf_op jit(solution)/shard_map/all_gather | solution.py:225
  353.6 8.0 fusion.27
  361.6 4.7 all-gather.1
  366.3 2.0 convolution_add_fusion.2
  368.4 2.4 fusion.26
  370.8 4.4 all-gather
  375.1 82.8 %all-gather.17.cloned.1.call-done = bf16[1280,5120]{1,0:T(8,128)(2,1)} async-done(((bf16[80,5120]{1,0:T(8,128)(2,1)}), bf16[1280,5120]{1,0:T(8,128)(2,1)}) %all-gather.17.cloned.1.call-update) | async-done | bytes 13107216 | tf_op jit(solution)/shard_map/all_gather | solution.py:229
  457.9 6.5 fusion.165
  464.5 97.8 %all-gather.19.cloned.1.call-done = bf16[1280,5120]{1,0:T(8,128)(2,1)} async-done(((bf16[80,5120]{1,0:T(8,128)(2,1)}), bf16[1280,5120]{1,0:T(8,128)(2,1)}) %all-gather.19.cloned.1.call-update) | async-done | bytes 13107216 | tf_op jit(solution)/shard_map/all_gather | solution.py:230
  562.3 10.5 fusion.49
  572.8 6.2 add_add_fusion
  579.1 12.6 fusion.53
  591.8 1.8 fusion.169
  593.6 9.9 multiply_reduce_fusion.3
  604.8 11.1 convert_reduce_fusion.1
  615.9 12.7 fusion.51
  628.6 16.2 %fusion.2 = bf16[1280,5120]{0,1:T(8,128)(2,1)} fusion(f32[5120,1280]{1,0:T(8,128)} %fusion.51, bf16[384,5120]{1,0:T(8,128)(2,1)} %get-tuple-element.137, bf16[2,1,384,1280]{3,2,1,0:T(8,128)(2,1)} %param.34), kind=kOutput, calls=%fused_computation.7 | convolution fusion | flops 5046272000 | bytes 44236800 | tf_op jit(solution)/shard_map/dot_general | solution.py:14
  644.8 17.6 %copy.89 = bf16[1280,5120]{1,0:T(8,128)(2,1)} copy(bf16[1280,5120]{0,1:T(8,128)(2,1)} %fusion.2) | data formatting | bytes 26214400
  663.7 2.1 slice_convert_fusion.1
  665.8 3.1 fusion.135
  670.4 14.2 convolution_convert_fusion.5
  684.5 13.5 convolution_convert_fusion.4
  698.0 8.3 all-reduce.15
  708.9 11.2 convert_reduce_fusion.3
  720.1 10.6 multiply_reduce_fusion.7
  730.7 9.7 convert_reduce_fusion.2
  740.5 10.3 multiply_reduce_fusion.6
  753.1 2.7 fusion.11
  757.7 3.0 convolution_convert_fusion.3
  760.8 1.9 copy.70
  762.6 3.0 convolution_convert_fusion.2
  769.5 2.2 convolution_bitcast_fusion.5
  771.7 3.2 convolution_bitcast_fusion.4
  774.9 2.4 fusion.133
  777.3 3.1 convolution_bitcast_fusion.2
  780.4 3.1 convolution_bitcast_fusion.1
  786.1 8.3 fusion.116
  794.5 11.1 add_convert_fusion.4
  806.7 12.7 fusion.185
  819.5 15.7 %add_convert_fusion.3 = bf16[1280,5120]{1,0:T(8,128)(2,1)} fusion(f32[1280,5120]{1,0:T(8,128)} %fusion.185, bf16[128,5120]{1,0:T(8,128)(2,1)} %copy-done.26, f32[128,1280]{1,0:T(8,128)S(1)} %copy-done.6, f32[128]{0:T(128)S(1)} %copy-done.75, f32[128]{0:T(128)S(1)} %copy-done.70, f32[1280]{0:T(1024)S(1)} %convert_element_type.331), kind=kOutput, calls=%fused_computation.5 | convolution fusion | flops 1691484160 | bytes 41293824 | tf_op jit(solution)/shard_map/dot_general | solution.py:14
  836.3 12.8 fusion.146
  849.1 16.3 %add_convert_fusion.2 = bf16[5120,1280]{1,0:T(8,128)(2,1)} fusion(f32[5120,1280]{1,0:T(8,128)} %fusion.146, f32[128,1280]{1,0:T(8,128)S(1)} %copy-done.22, f32[128,5120]{1,0:T(8,128)} %convolution_add_fusion.1), kind=kOutput, calls=%fused_computation.4 | convolution fusion | flops 1696890880 | bytes 42598400 | tf_op jit(solution)/shard_map/dot_general | solution.py:14
  866.1 13.9 fusion.167
  880.0 19.8 %add_convert_fusion.1 = bf16[1280,5120]{1,0:T(8,128)(2,1)} fusion(f32[1280,5120]{1,0:T(8,128)} %fusion.167, f32[2,5120]{1,0:T(2,128)S(1)} %fusion.134, bf16[2,1,1280]{2,1,0:T(2,128)(2,1)S(1)} %copy-done.61), kind=kOutput, calls=%fused_computation.3 | convolution fusion | flops 170393600 | bytes 39367680 | tf_op jit(solution)/shard_map/dot_general | solution.py:188
  901.2 2.3 copy.90
  903.5 83.3 %reduce-scatter.9.cloned.1.call-done = bf16[80,3840]{1,0:T(8,128)(2,1)} async-done(((bf16[1280,3840]{1,0:T(8,128)(2,1)}), bf16[80,3840]{1,0:T(8,128)(2,1)}) %reduce-scatter.9.cloned.1.call-update) | async-done | bytes 614416 | tf_op jit(solution)/shard_map/reduce_scatter | solution.py:266
  986.8 142.1 %reduce-scatter.13.cloned.1.call-done = bf16[80,5120]{1,0:T(8,128)(2,1)} async-done(((bf16[1280,5120]{1,0:T(8,128)(2,1)}), bf16[80,5120]{1,0:T(8,128)(2,1)}) %reduce-scatter.13.cloned.1.call-update) | async-done | bytes 819216 | tf_op jit(solution)/shard_map/reduce_scatter | solution.py:272
  1128.9 142.2 %reduce-scatter.15.cloned.1.call-done = bf16[320,1280]{1,0:T(8,128)(2,1)} async-done(((bf16[5120,1280]{1,0:T(8,128)(2,1)}), bf16[320,1280]{1,0:T(8,128)(2,1)}) %reduce-scatter.15.cloned.1.call-update) | async-done | bytes 819216 | tf_op jit(solution)/shard_map/reduce_scatter | solution.py:275
  1271.1 141.5 %reduce-scatter.17.cloned.1.call-done = bf16[80,5120]{1,0:T(8,128)(2,1)} async-done(((bf16[1280,5120]{1,0:T(8,128)(2,1)}), bf16[80,5120]{1,0:T(8,128)(2,1)}) %reduce-scatter.17.cloned.1.call-update) | async-done | bytes 819216 | tf_op jit(solution)/shard_map/reduce_scatter | solution.py:287
  1412.6 7.2 fusion.194
  1419.9 8.4 fusion.81
  1428.5 59.6 %all-reduce.12 = (bf16[1280]{0:T(1024)(128)(2,1)S(1)}, bf16[1280]{0:T(1024)(128)(2,1)S(1)}, bf16[5120]{0:T(1024)(128)(2,1)S(1)}, bf16[5120]{0:T(1024)(128)(2,1)S(1)}, bf16[5120]{0:T(1024)(128)(2,1)S(1)}) all-reduce(bf16[1280]{0:T(1024)(128)(2,1)S(1)} %add_convert_fusion.9, ...), channel_id=8, replica_groups=mesh['dp'=16,'query'=2] {'dp'}, use_global_device_ids=true, to_apply=%region_36.37.clone | all-reduce | flops 17920 | bytes 71680
  1488.5 5.0 all-reduce.14
  1497.2 1.6 fusion.80
  1499.9 33.9 %all-reduce.19.cloned.1.call-done = (bf16[80,5120]{0,1:T(8,128)(2,1)}, bf16[80,3840]{1,0:T(8,128)(2,1)}, bf16[80,1280]{1,0:T(8,128)(2,1)}, bf16[80,5120]{1,0:T(8...) async-done(((bf16[80,5120]{0,1:T(8,128)(2,1)}, bf16[80,3840]{1,0:T(8,128)(2,1)}, bf16[80,1280]{1,0:T(8,128)(2,1)}, bf16[80,5120]{1,0:T(8,128)(2,1)}, ...) | async-done | bytes 4096016 | tf_op jit(solution)/shard_map/psum | solution.py:309
  1533.8 2.6 convert_element_type.387
  (319 shorter events, 46.4 us)
Async XLA Ops:
  7.2 72.5 %copy-start.85 = (s32[1,2,1]{1,2,0:T(1,128)S(1)}, s32[1,2,1]{1,2,0:T(1,128)}, u32[]{:S(2)}) copy-start(s32[1,2,1]{1,2,0:T(1,128)} %param.37) | copy-start | bytes 28
  7.3 73.1 %copy-start.82 = (s32[2,1,384]{2,1,0:T(1,128)S(1)}, s32[2,1,384]{2,1,0:T(1,128)}, u32[]{:S(2)}) copy-start(s32[2,1,384]{2,1,0:T(1,128)} %param.35) | copy-start | bytes 9220
  7.3 73.1 %copy-start.83 = (s32[2,1,384]{2,1,0:T(1,128)S(1)}, s32[2,1,384]{2,1,0:T(1,128)}, u32[]{:S(2)}) copy-start(s32[2,1,384]{2,1,0:T(1,128)} %param.36) | copy-start | bytes 9220
  7.3 73.2 %copy-start.7 = (bf16[2,1,128,1280]{3,2,1,0:T(8,128)(2,1)S(1)}, bf16[2,1,128,1280]{3,2,1,0:T(8,128)(2,1)}, u32[]{:S(2)}) copy-start(bf16[2,1,128,1280]{3,2,1,0:T(8,128)(2,1)} %param.21) | copy-start | bytes 1966084
  7.3 90.3 %all-gather.9.cloned.1.call-start = ((), (), s32[]{:S(2)}) async-start(), calls=%async_computation.6 | async-start | bytes 10444800 | tf_op jit(solution)/shard_map/all_gather | solution.py:222
  8.0 136.1 %all-gather.11.cloned.1.call-start = ((), (), s32[]{:S(2)}) async-start(), calls=%async_computation.7 | async-start | bytes 3481600 | tf_op jit(solution)/shard_map/all_gather | solution.py:223
  8.8 240.5 %all-gather.13.cloned.1.call-start = ((), (), s32[]{:S(2)}) async-start(), calls=%async_computation.8 | async-start | bytes 13926400 | tf_op jit(solution)/shard_map/all_gather | solution.py:224
  9.5 344.1 %all-gather.15.cloned.1.call-start = ((), (), s32[]{:S(2)}) async-start(), calls=%async_computation.9 | async-start | bytes 13926400 | tf_op jit(solution)/shard_map/all_gather | solution.py:225
  10.1 447.9 %all-gather.17.cloned.1.call-start = ((), (), s32[]{:S(2)}) async-start(), calls=%async_computation.10 | async-start | bytes 13926400 | tf_op jit(solution)/shard_map/all_gather | solution.py:229
  10.7 551.6 %all-gather.19.cloned.1.call-start = ((), (), s32[]{:S(2)}) async-start(), calls=%async_computation.11 | async-start | bytes 13926400 | tf_op jit(solution)/shard_map/all_gather | solution.py:230
  11.2 889.9 %reduce-scatter.19.cloned.1.call-start = ((), (), s32[]{:S(2)}) async-start(), calls=%async_computation.17 | async-start | bytes 13926400
  79.8 23.9 %copy-start.43 = (f32[1280]{0:T(1024)}, f32[1280]{0:T(1024)S(1)}, u32[]{:S(2)}) copy-start(f32[1280]{0:T(1024)S(1)} %convert_element_type.325) | copy-start | bytes 15364
  80.6 22.3 %copy-start.76 = (f32[128]{0:T(128)}, f32[128]{0:T(128)S(1)}, u32[]{:S(2)}) copy-start(f32[128]{0:T(128)S(1)} %get-tuple-element.159) | copy-start | bytes 1540
  80.6 23.0 %copy-start.71 = (f32[128]{0:T(128)}, f32[128]{0:T(128)S(1)}, u32[]{:S(2)}) copy-start(f32[128]{0:T(128)S(1)} %get-tuple-element.160) | copy-start | bytes 1540
  81.0 22.0 %copy-start.80 = (f32[128]{0:T(128)}, f32[128]{0:T(128)S(1)}, u32[]{:S(2)}) copy-start(f32[128]{0:T(128)S(1)} %add_rsqrt_fusion.1) | copy-start | bytes 1540
  81.0 22.6 %copy-start.78 = (f32[128]{0:T(128)}, f32[128]{0:T(128)S(1)}, u32[]{:S(2)}) copy-start(f32[128]{0:T(128)S(1)} %add_rsqrt_fusion.3) | copy-start | bytes 1540
  112.9 34.1 %copy-start.38 = (bf16[20,64,128]{2,1,0:T(8,128)(2,1)}, bf16[20,64,128]{2,1,0:T(8,128)(2,1)S(1)}, u32[]{:S(2)}) copy-start(bf16[20,64,128]{2,1,0:T(8,128)(2,1)S(1)} %convolution_convert_fusion.6) | copy-start | bytes 983044
  146.8 605.1 %copy-start.5 = (f32[128,1280]{1,0:T(8,128)}, f32[128,1280]{1,0:T(8,128)S(1)}, u32[]{:S(2)}) copy-start(f32[128,1280]{1,0:T(8,128)S(1)} %get-tuple-element.146) | copy-start | bytes 1966084
  146.8 102.5 %copy-start.69 = (f32[128]{0:T(128)}, f32[128]{0:T(128)S(1)}, u32[]{:S(2)}) copy-start(f32[128]{0:T(128)S(1)} %broadcast_multiply_fusion.8) | copy-start | bytes 1540
  150.7 589.7 %copy-start.9 = (f32[128,1280]{1,0:T(8,128)}, f32[128,1280]{1,0:T(8,128)S(1)}, u32[]{:S(2)}) copy-start(f32[128,1280]{1,0:T(8,128)S(1)} %get-tuple-element.150) | copy-start | bytes 1966084
  151.0 106.5 %copy-start.74 = (f32[128]{0:T(128)}, f32[128]{0:T(128)S(1)}, u32[]{:S(2)}) copy-start(f32[128]{0:T(128)S(1)} %add_rsqrt_fusion) | copy-start | bytes 1540
  353.6 12.7 copy-start
  353.6 14.7 slice-start.4
  353.6 14.7 slice-start.5
  353.6 14.7 slice-start.6
  366.3 91.6 %copy-start.60 = (bf16[2,1,1280]{2,1,0:T(2,128)(2,1)}, bf16[2,1,1280]{2,1,0:T(2,128)(2,1)S(1)}, u32[]{:S(2)}) copy-start(bf16[2,1,1280]{2,1,0:T(2,128)(2,1)S(1)} %all-gather.1) | copy-start | bytes 15364
  370.8 93.7 %copy-start.47 = (bf16[128,1280]{1,0:T(8,128)(2,1)}, bf16[128,1280]{1,0:T(8,128)(2,1)S(1)}, u32[]{:S(2)}) copy-start(bf16[128,1280]{1,0:T(8,128)(2,1)S(1)} %fusion.26) | copy-start | bytes 983044
  375.1 216.6 %copy-start.62 = (bf16[2,1,1280]{2,1,0:T(2,128)(2,1)}, bf16[2,1,1280]{2,1,0:T(2,128)(2,1)S(1)}, u32[]{:S(2)}) copy-start(bf16[2,1,1280]{2,1,0:T(2,128)(2,1)S(1)} %all-gather) | copy-start | bytes 15364
  572.8 18.9 %slice-start = ((s8[13107200]{0:T(1024)(128)(4,1)}), s8[4194304]{0:T(1024)(128)(4,1)S(1)}, s32[]{:S(2)}) async-start(s8[13107200]{0:T(1024)(128)(4,1)} %bitcast.251), calls=%async_computation.19 | async-start | bytes 8388608
  572.8 18.9 %slice-start.1 = ((s8[13107200]{0:T(1024)(128)(4,1)}), s8[4194304]{0:T(1024)(128)(4,1)S(1)}, s32[]{:S(2)}) async-start(s8[13107200]{0:T(1024)(128)(4,1)} %bitcast.251), calls=%async_computation.20 | async-start | bytes 8388608
  579.1 12.7 slice-start.2
  579.1 12.7 slice-start.3
  615.9 12.7 copy-start.4
  662.5 241.1 %reduce-scatter.11.cloned.1.call-start = ((), (), s32[]{:S(2)}) async-start(), calls=%async_computation.13 | async-start | bytes 3481600 | tf_op jit(solution)/shard_map/reduce_scatter | solution.py:269
  707.9 44.0 %copy-start.21 = (f32[128,1280]{1,0:T(8,128)}, f32[128,1280]{1,0:T(8,128)S(1)}, u32[]{:S(2)}) copy-start(f32[128,1280]{1,0:T(8,128)S(1)} %scatter-add.9) | copy-start | bytes 1966084
  708.9 31.6 %copy-start.23 = (f32[128,1280]{1,0:T(8,128)}, f32[128,1280]{1,0:T(8,128)S(1)}, u32[]{:S(2)}) copy-start(f32[128,1280]{1,0:T(8,128)S(1)} %scatter-add.6) | copy-start | bytes 1966084
  720.1 10.6 copy-start.25
  720.1 10.6 copy-start.11
  730.7 9.8 copy-start.70
  730.7 9.8 copy-start.75
  740.5 10.4 copy-start.26
  740.5 10.4 copy-start.34
  755.8 231.0 %reduce-scatter.9.cloned.1.call-start = ((), (), s32[]{:S(2)}) async-start(), calls=%async_computation.12 | async-start | bytes 10444800 | tf_op jit(solution)/shard_map/reduce_scatter | solution.py:266
  785.4 9.1 copy-start.27
  786.1 8.4 copy-start.77
  786.1 8.4 copy-start.81
  805.6 13.8 copy-start.6
  805.7 323.3 %reduce-scatter.13.cloned.1.call-start = ((), (), s32[]{:S(2)}) async-start(), calls=%async_computation.14 | async-start | bytes 13926400 | tf_op jit(solution)/shard_map/reduce_scatter | solution.py:272
  835.2 13.9 copy-start.22
  835.2 435.9 %reduce-scatter.15.cloned.1.call-start = ((), (), s32[]{:S(2)}) async-start(), calls=%async_computation.15 | async-start | bytes 13926400 | tf_op jit(solution)/shard_map/reduce_scatter | solution.py:275
  865.4 14.6 copy-start.61
  865.4 547.1 %reduce-scatter.17.cloned.1.call-start = ((), (), s32[]{:S(2)}) async-start(), calls=%async_computation.16 | async-start | bytes 13926400 | tf_op jit(solution)/shard_map/reduce_scatter | solution.py:287
  899.8 633.9 %all-reduce.19.cloned.1.call-start = ((), (), s32[]{:S(2)}) async-start(), calls=%async_computation.18 | async-start | bytes 9175040 | tf_op jit(solution)/shard_map/psum | solution.py:309
  1419.8 8.5 copy-start.32
  1419.8 8.5 copy-start.68
  1419.8 8.5 copy-start.73
  1419.8 8.6 copy-start.58
  1419.8 8.6 copy-start.59
  1419.9 8.6 copy-start.56
  1419.9 8.6 copy-start.57
  1419.9 76.4 %copy-start.46 = (bf16[128,1280]{1,0:T(8,128)(2,1)S(1)}, bf16[128,1280]{1,0:T(8,128)(2,1)}, u32[]{:S(2)}) copy-start(bf16[128,1280]{1,0:T(8,128)(2,1)} %copy-done.45) | copy-start | bytes 983044
  1419.9 76.4 %copy-start.48 = (bf16[128,1280]{1,0:T(8,128)(2,1)S(1)}, bf16[128,1280]{1,0:T(8,128)(2,1)}, u32[]{:S(2)}) copy-start(bf16[128,1280]{1,0:T(8,128)(2,1)} %copy-done.47) | copy-start | bytes 983044
  1419.9 77.3 %copy-start.18 = (f32[128,1280]{1,0:T(8,128)S(1)}, f32[128,1280]{1,0:T(8,128)}, u32[]{:S(2)}) copy-start(f32[128,1280]{1,0:T(8,128)} %copy-done.17) | copy-start | bytes 1966084
  1419.9 77.2 %copy-start.20 = (f32[128,1280]{1,0:T(8,128)S(1)}, f32[128,1280]{1,0:T(8,128)}, u32[]{:S(2)}) copy-start(f32[128,1280]{1,0:T(8,128)} %copy-done.19) | copy-start | bytes 1966084
  (49 other events, 146.2 us)
Sparse Core Ops, SparseCore 0:
  10.4 87.1 all-gather.8
  99.9 44.1 all-gather.10
  146.4 102.8 all-gather.12
  251.4 102.1 all-gather.14
  355.7 102.1 all-gather.16
  460.1 102.1 all-gather.18
  662.6 136.5 reduce-scatter.18
  803.4 65.9 reduce-scatter.10
  873.6 113.2 reduce-scatter.8
  990.8 138.1 reduce-scatter.12
  1133.6 137.4 reduce-scatter.14
  1275.1 137.4 reduce-scatter.16
  1416.4 117.3 all-reduce.18
where the time goes:
time: 1560 us; the launch traced here: 1550 us
  waiting for transfers between devices  969 us (62%)
  matrix products  339 us (22%)
  blocking collectives  147 us (9%)
  local copies, waits for them, and re-layouts  41 us (3%)
  other arithmetic  33.2 us (2%)
  between operations  18 us (1%)
    reduce_scatter x1, waiting for transfers between devices, shards(): lax.psum_scatter(totals[3].astype(jnp.bfloat16), 'dp', scatter_dimension=...  142 us
    reduce_scatter x1, waiting for transfers between devices, shards(): lax.psum_scatter(totals[2].astype(jnp.bfloat16), 'dp', scatter_dimension=...  142 us
    reduce_scatter x1, waiting for transfers between devices, shards(): lax.psum_scatter(totals[7].astype(jnp.bfloat16), 'dp', scatter_dimension=...  141 us
    unnamed x3, blocking collectives  133 us
    dot_general x10, matrix products, row_product(): lax.dot_general(left, right, (((0,), (0,)), ((), ())), preferred_element_...  110 us
    all_gather x1, waiting for transfers between devices, shards(): lax.all_gather(up_weight, 'dp', axis=0, tiled=True)  98.3 us
    all_gather x1, waiting for transfers between devices, shards(): lax.all_gather(gene_weight, 'dp', axis=0, tiled=True)  97.8 us
    all_gather x1, waiting for transfers between devices, shards(): lax.all_gather(down_weight, 'dp', axis=0, tiled=True)  96.1 us
  transfers between devices with their start and end apart: 13, of which 11 were waited for; matrix products, arithmetic and copies ran while one was open for 19% of the time, Pallas kernels for 0%

commit v1 on v0

--- a/solution.py
+++ b/solution.py
@@ -213,6 +213,10 @@
     query_label,
     query_live,
 ):
+
+    def serve_zone(message, a_name):
+        return lax.all_gather(message, a_name).sum(axis=0)
+
     micro_count = tokens.shape[0]
     outputs = []
     input_grads = []
@@ -306,7 +310,7 @@
         lax.psum(owned[5].astype(jnp.bfloat16), "query").astype(jnp.float32),
         lax.psum(owned[6].astype(jnp.bfloat16), "query").astype(jnp.float32),
         lax.psum(owned[7].astype(jnp.bfloat16), "query").astype(jnp.float32),
-        lax.psum(owned[8].astype(jnp.bfloat16), "query").astype(jnp.float32),
+        serve_zone(owned[8].astype(jnp.bfloat16), "query").astype(jnp.float32),
         lax.psum(owned[9].astype(jnp.bfloat16), "query").astype(jnp.float32),
         lax.psum(owned[10].astype(jnp.bfloat16), "query").astype(jnp.float32),
     )

time: 1560 us -> 1560 us (level)
    unnamed x222 -> x214, local copies, waits for them, and re-layouts: 34.9 us -> 31 us
  transfers between devices with their start and end apart: 13 -> 14, of which waited for: 11 -> 11; matrix products, arithmetic and copies ran while one was open for 19% -> 19% of each run, Pallas kernels for 0% -> 0%
where the time goes in v1:
time: 1560 us; the launch traced here: 1550 us
  waiting for transfers between devices  964 us (62%)
  matrix products  342 us (22%)
  blocking collectives  147 us (9%)
  other arithmetic  37.6 us (2%)
  local copies, waits for them, and re-layouts  37.2 us (2%)
  between operations  18 us (1%)
    reduce_scatter x1, waiting for transfers between devices, shards(): lax.psum_scatter(totals[7].astype(jnp.bfloat16), 'dp', scatter_dimension=...  142 us
    reduce_scatter x1, waiting for transfers between devices, shards(): lax.psum_scatter(totals[3].astype(jnp.bfloat16), 'dp', scatter_dimension=...  142 us
    reduce_scatter x1, waiting for transfers between devices, shards(): lax.psum_scatter(totals[2].astype(jnp.bfloat16), 'dp', scatter_dimension=...  141 us
    unnamed x3, blocking collectives  133 us
    dot_general x10, matrix products, row_product(): lax.dot_general(left, right, (((0,), (0,)), ((), ())), preferred_element_...  113 us
    all_gather x1, waiting for transfers between devices, shards(): lax.all_gather(up_weight, 'dp', axis=0, tiled=True)  98.3 us
    all_gather x1, waiting for transfers between devices, shards(): lax.all_gather(gene_weight, 'dp', axis=0, tiled=True)  97.8 us
    all_gather x1, waiting for transfers between devices, shards(): lax.all_gather(down_weight, 'dp', axis=0, tiled=True)  96.1 us
  transfers between devices with their start and end apart: 14, of which 11 were waited for; matrix products, arithmetic and copies ran while one was open for 19% of the time, Pallas kernels for 0%

profile of v1, /device:TPU:0, one launch (start us, length us, event | category | flops | bytes accessed | tf_op | source)
XLA Modules:
  0.0 1547.1 jit_solution(2406345532875629870)
XLA Ops:
  14.5 65.3 %all-reduce.13 = (bf16[1280]{0:T(1024)(128)(2,1)S(1)}, bf16[5120]{0:T(1024)(128)(2,1)S(1)}, bf16[1280]{0:T(1024)(128)(2,1)S(1)}, bf16[5120]{0:T(1024)(128)(2,1)S(1)}, bf16[5120]{0:T(1024)(128)(2,1)S(1)}) all-reduce(bf16[1280]{0:T(1024)(128)(2,1)S(1)} %dynamic-update-slice.6, ...), channel_id=1, replica_groups=mesh['dp'=16,'query'=2] {'dp'}, use_global_device_ids=true, to_apply=%add | all-reduce | flops 17920 | bytes 71680
  81.0 16.6 %all-gather.11.cloned.1.call-done = bf16[1280,3840]{1,0:T(8,128)(2,1)} async-done(((bf16[80,3840]{1,0:T(8,128)(2,1)}), bf16[1280,3840]{1,0:T(8,128)(2,1)}) %all-gather.11.cloned.1.call-update) | async-done | bytes 9830416 | tf_op jit(solution)/shard_map/all_gather | solution.py:226
  97.6 5.3 convolution_convert_fusion
  103.7 5.9 convolution_convert_fusion.1
  112.9 31.2 %all-gather.13.cloned.1.call-done = bf16[1280,1280]{1,0:T(8,128)(2,1)} async-done(((bf16[80,1280]{1,0:T(8,128)(2,1)}), bf16[1280,1280]{1,0:T(8,128)(2,1)}) %all-gather.13.cloned.1.call-update) | async-done | bytes 3276816 | tf_op jit(solution)/shard_map/all_gather | solution.py:227
  144.1 2.7 fusion.191
  151.0 98.3 %all-gather.15.cloned.1.call-done = bf16[1280,5120]{1,0:T(8,128)(2,1)} async-done(((bf16[80,5120]{1,0:T(8,128)(2,1)}), bf16[1280,5120]{1,0:T(8,128)(2,1)}) %all-gather.15.cloned.1.call-update) | async-done | bytes 13107216 | tf_op jit(solution)/shard_map/all_gather | solution.py:228
  249.3 8.2 convolution_add_fusion.1
  257.5 96.1 %all-gather.17.cloned.1.call-done = bf16[5120,1280]{1,0:T(8,128)(2,1)} async-done(((bf16[320,1280]{1,0:T(8,128)(2,1)}), bf16[5120,1280]{1,0:T(8,128)(2,1)}) %all-gather.17.cloned.1.call-update) | async-done | bytes 13107216 | tf_op jit(solution)/shard_map/all_gather | solution.py:229
  353.6 8.0 fusion.27
  361.6 4.7 all-gather.2
  366.3 2.0 convolution_add_fusion.2
  368.4 2.4 fusion.26
  370.8 4.4 all-gather.1
  375.1 82.8 %all-gather.19.cloned.1.call-done = bf16[1280,5120]{1,0:T(8,128)(2,1)} async-done(((bf16[80,5120]{1,0:T(8,128)(2,1)}), bf16[1280,5120]{1,0:T(8,128)(2,1)}) %all-gather.19.cloned.1.call-update) | async-done | bytes 13107216 | tf_op jit(solution)/shard_map/all_gather | solution.py:233
  457.9 6.5 fusion.165
  464.5 97.8 %all-gather.21.cloned.1.call-done = bf16[1280,5120]{1,0:T(8,128)(2,1)} async-done(((bf16[80,5120]{1,0:T(8,128)(2,1)}), bf16[1280,5120]{1,0:T(8,128)(2,1)}) %all-gather.21.cloned.1.call-update) | async-done | bytes 13107216 | tf_op jit(solution)/shard_map/all_gather | solution.py:234
  562.3 10.4 fusion.49
  572.7 6.2 add_add_fusion
  579.0 12.6 fusion.53
  591.7 1.8 fusion.169
  593.5 9.9 multiply_reduce_fusion.3
  604.7 11.1 convert_reduce_fusion.1
  615.8 12.7 fusion.51
  628.5 16.2 %fusion.2 = bf16[1280,5120]{0,1:T(8,128)(2,1)} fusion(f32[5120,1280]{1,0:T(8,128)} %fusion.51, bf16[384,5120]{1,0:T(8,128)(2,1)} %get-tuple-element.136, bf16[2,1,384,1280]{3,2,1,0:T(8,128)(2,1)} %param.34), kind=kOutput, calls=%fused_computation.7 | convolution fusion | flops 5046272000 | bytes 44236800 | tf_op jit(solution)/shard_map/dot_general | solution.py:14
  644.7 17.6 %copy.88 = bf16[1280,5120]{1,0:T(8,128)(2,1)} copy(bf16[1280,5120]{0,1:T(8,128)(2,1)} %fusion.2) | data formatting | bytes 26214400
  663.6 2.1 slice_convert_fusion.1
  665.7 3.1 fusion.135
  670.3 14.1 convolution_convert_fusion.5
  684.4 13.5 convolution_convert_fusion.4
  697.9 8.3 all-reduce.15
  708.8 11.2 convert_reduce_fusion.3
  720.0 10.6 multiply_reduce_fusion.7
  730.6 9.7 convert_reduce_fusion.2
  740.4 10.3 multiply_reduce_fusion.6
  753.0 2.7 fusion.11
  757.7 3.0 convolution_convert_fusion.3
  760.7 1.9 copy.69
  762.6 3.0 convolution_convert_fusion.2
  769.4 2.2 convolution_bitcast_fusion.5
  771.6 3.2 convolution_bitcast_fusion.4
  774.8 2.4 fusion.133
  777.3 3.1 convolution_bitcast_fusion.2
  780.4 3.1 convolution_bitcast_fusion.1
  786.1 8.4 fusion.116
  794.5 11.1 add_convert_fusion.4
  806.7 13.3 fusion.146
  820.0 15.7 %add_convert_fusion.2 = bf16[5120,1280]{1,0:T(8,128)(2,1)} fusion(f32[5120,1280]{1,0:T(8,128)} %fusion.146, f32[128,1280]{1,0:T(8,128)S(1)} %copy-done.22, f32[128,5120]{1,0:T(8,128)} %convolution_add_fusion.1), kind=kOutput, calls=%fused_computation.4 | convolution fusion | flops 1696890880 | bytes 42598400 | tf_op jit(solution)/shard_map/dot_general | solution.py:14
  836.4 13.8 fusion.167
  850.3 17.7 %add_convert_fusion.1 = bf16[1280,5120]{1,0:T(8,128)(2,1)} fusion(f32[1280,5120]{1,0:T(8,128)} %fusion.167, f32[2,5120]{1,0:T(2,128)S(1)} %fusion.134, bf16[2,1,1280]{2,1,0:T(2,128)(2,1)S(1)} %copy-done.58), kind=kOutput, calls=%fused_computation.3 | convolution fusion | flops 170393600 | bytes 39367680 | tf_op jit(solution)/shard_map/dot_general | solution.py:188
  869.1 13.0 fusion.185
  882.0 18.8 %add_convert_fusion.3 = bf16[1280,5120]{1,0:T(8,128)(2,1)} fusion(f32[1280,5120]{1,0:T(8,128)} %fusion.185, bf16[128,5120]{1,0:T(8,128)(2,1)} %copy-done.26, f32[128,1280]{1,0:T(8,128)S(1)} %copy-done.6, f32[128]{0:T(128)S(1)} %copy-done.72, f32[128]{0:T(128)S(1)} %copy-done.67, f32[1280]{0:T(1024)S(1)} %convert_element_type.333), kind=kOutput, calls=%fused_computation.5 | convolution fusion | flops 1691484160 | bytes 41293824 | tf_op jit(solution)/shard_map/dot_general | solution.py:14
  902.9 8.8 fusion.194
  911.7 75.1 %reduce-scatter.9.cloned.1.call-done = bf16[80,3840]{1,0:T(8,128)(2,1)} async-done(((bf16[1280,3840]{1,0:T(8,128)(2,1)}), bf16[80,3840]{1,0:T(8,128)(2,1)}) %reduce-scatter.9.cloned.1.call-update) | async-done | bytes 614416 | tf_op jit(solution)/shard_map/reduce_scatter | solution.py:270
  986.8 142.1 %reduce-scatter.15.cloned.1.call-done = bf16[320,1280]{1,0:T(8,128)(2,1)} async-done(((bf16[5120,1280]{1,0:T(8,128)(2,1)}), bf16[320,1280]{1,0:T(8,128)(2,1)}) %reduce-scatter.15.cloned.1.call-update) | async-done | bytes 819216 | tf_op jit(solution)/shard_map/reduce_scatter | solution.py:279
  1128.9 142.2 %reduce-scatter.17.cloned.1.call-done = bf16[80,5120]{1,0:T(8,128)(2,1)} async-done(((bf16[1280,5120]{1,0:T(8,128)(2,1)}), bf16[80,5120]{1,0:T(8,128)(2,1)}) %reduce-scatter.17.cloned.1.call-update) | async-done | bytes 819216 | tf_op jit(solution)/shard_map/reduce_scatter | solution.py:291
  1271.1 141.5 %reduce-scatter.13.cloned.1.call-done = bf16[80,5120]{1,0:T(8,128)(2,1)} async-done(((bf16[1280,5120]{1,0:T(8,128)(2,1)}), bf16[80,5120]{1,0:T(8,128)(2,1)}) %reduce-scatter.13.cloned.1.call-update) | async-done | bytes 819216 | tf_op jit(solution)/shard_map/reduce_scatter | solution.py:276
  1412.7 8.3 fusion.81
  1421.1 59.6 %all-reduce.12 = (bf16[1280]{0:T(1024)(128)(2,1)S(1)}, bf16[1280]{0:T(1024)(128)(2,1)S(1)}, bf16[5120]{0:T(1024)(128)(2,1)S(1)}, bf16[5120]{0:T(1024)(128)(2,1)S(1)}, bf16[5120]{0:T(1024)(128)(2,1)S(1)}) all-reduce(bf16[1280]{0:T(1024)(128)(2,1)S(1)} %add_convert_fusion.9, ...), channel_id=9, replica_groups=mesh['dp'=16,'query'=2] {'dp'}, use_global_device_ids=true, to_apply=%region_36.37.clone | all-reduce | flops 17920 | bytes 71680
  1481.1 5.0 all-reduce.14
  1488.8 1.9 maximum_bitcast_fusion.1
  1493.6 2.0 reduce_sum.328
  1496.9 36.4 %all-reduce.19.cloned.1.call-done = (bf16[80,3840]{1,0:T(8,128)(2,1)}, bf16[80,1280]{1,0:T(8,128)(2,1)}, bf16[80,5120]{1,0:T(8,128)(2,1)}, bf16[320,1280]{1,0:T(8,128)(2,1)}, bf16[80,5120]{1,0:T(8,128)(2,1)}) async-done(((bf16[80,3840]{1,0:T(8,128)(2,1)}, bf16[80,1280]{1,0:T(8,128)(2,1)}, bf16[80,5120]{1,0:T(8,128)(2,1)}, bf16[320,1280]{1,0:T(8,128)(2,1)}, bf16[80,5120]{1,0:T(8,128)(2,1)}), ...) | async-done | bytes 3276816 | tf_op jit(solution)/shard_map/psum | solution.py:305
  1533.3 2.6 convert_element_type.389
  (316 shorter events, 47.7 us)
Async XLA Ops:
  7.2 72.5 %copy-start.82 = (s32[1,2,1]{1,2,0:T(1,128)S(1)}, s32[1,2,1]{1,2,0:T(1,128)}, u32[]{:S(2)}) copy-start(s32[1,2,1]{1,2,0:T(1,128)} %param.37) | copy-start | bytes 28
  7.3 73.1 %copy-start.79 = (s32[2,1,384]{2,1,0:T(1,128)S(1)}, s32[2,1,384]{2,1,0:T(1,128)}, u32[]{:S(2)}) copy-start(s32[2,1,384]{2,1,0:T(1,128)} %param.35) | copy-start | bytes 9220
  7.3 73.1 %copy-start.80 = (s32[2,1,384]{2,1,0:T(1,128)S(1)}, s32[2,1,384]{2,1,0:T(1,128)}, u32[]{:S(2)}) copy-start(s32[2,1,384]{2,1,0:T(1,128)} %param.36) | copy-start | bytes 9220
  7.3 73.2 %copy-start.7 = (bf16[2,1,128,1280]{3,2,1,0:T(8,128)(2,1)S(1)}, bf16[2,1,128,1280]{3,2,1,0:T(8,128)(2,1)}, u32[]{:S(2)}) copy-start(bf16[2,1,128,1280]{3,2,1,0:T(8,128)(2,1)} %param.21) | copy-start | bytes 1966084
  7.3 90.3 %all-gather.11.cloned.1.call-start = ((), (), s32[]{:S(2)}) async-start(), calls=%async_computation.6 | async-start | bytes 10444800 | tf_op jit(solution)/shard_map/all_gather | solution.py:226
  8.0 136.1 %all-gather.13.cloned.1.call-start = ((), (), s32[]{:S(2)}) async-start(), calls=%async_computation.7 | async-start | bytes 3481600 | tf_op jit(solution)/shard_map/all_gather | solution.py:227
  8.8 240.5 %all-gather.15.cloned.1.call-start = ((), (), s32[]{:S(2)}) async-start(), calls=%async_computation.8 | async-start | bytes 13926400 | tf_op jit(solution)/shard_map/all_gather | solution.py:228
  9.5 344.1 %all-gather.17.cloned.1.call-start = ((), (), s32[]{:S(2)}) async-start(), calls=%async_computation.9 | async-start | bytes 13926400 | tf_op jit(solution)/shard_map/all_gather | solution.py:229
  10.1 447.9 %all-gather.19.cloned.1.call-start = ((), (), s32[]{:S(2)}) async-start(), calls=%async_computation.10 | async-start | bytes 13926400 | tf_op jit(solution)/shard_map/all_gather | solution.py:233
  10.7 551.6 %all-gather.21.cloned.1.call-start = ((), (), s32[]{:S(2)}) async-start(), calls=%async_computation.11 | async-start | bytes 13926400 | tf_op jit(solution)/shard_map/all_gather | solution.py:234
  11.2 889.6 %reduce-scatter.19.cloned.1.call-start = ((), (), s32[]{:S(2)}) async-start(), calls=%async_computation.18 | async-start | bytes 13926400 | tf_op jit(solution)/shard_map/reduce_scatter | solution.py:294
  79.8 23.9 %copy-start.41 = (f32[1280]{0:T(1024)}, f32[1280]{0:T(1024)S(1)}, u32[]{:S(2)}) copy-start(f32[1280]{0:T(1024)S(1)} %convert_element_type.327) | copy-start | bytes 15364
  80.6 22.3 %copy-start.73 = (f32[128]{0:T(128)}, f32[128]{0:T(128)S(1)}, u32[]{:S(2)}) copy-start(f32[128]{0:T(128)S(1)} %get-tuple-element.158) | copy-start | bytes 1540
  80.6 23.0 %copy-start.68 = (f32[128]{0:T(128)}, f32[128]{0:T(128)S(1)}, u32[]{:S(2)}) copy-start(f32[128]{0:T(128)S(1)} %get-tuple-element.159) | copy-start | bytes 1540
  81.0 22.0 %copy-start.77 = (f32[128]{0:T(128)}, f32[128]{0:T(128)S(1)}, u32[]{:S(2)}) copy-start(f32[128]{0:T(128)S(1)} %add_rsqrt_fusion.1) | copy-start | bytes 1540
  81.0 22.6 %copy-start.75 = (f32[128]{0:T(128)}, f32[128]{0:T(128)S(1)}, u32[]{:S(2)}) copy-start(f32[128]{0:T(128)S(1)} %add_rsqrt_fusion.3) | copy-start | bytes 1540
  112.9 34.2 %copy-start.36 = (bf16[20,64,128]{2,1,0:T(8,128)(2,1)}, bf16[20,64,128]{2,1,0:T(8,128)(2,1)S(1)}, u32[]{:S(2)}) copy-start(bf16[20,64,128]{2,1,0:T(8,128)(2,1)S(1)} %convolution_convert_fusion.6) | copy-start | bytes 983044
  146.8 605.0 %copy-start.5 = (f32[128,1280]{1,0:T(8,128)}, f32[128,1280]{1,0:T(8,128)S(1)}, u32[]{:S(2)}) copy-start(f32[128,1280]{1,0:T(8,128)S(1)} %get-tuple-element.145) | copy-start | bytes 1966084
  146.8 102.5 %copy-start.66 = (f32[128]{0:T(128)}, f32[128]{0:T(128)S(1)}, u32[]{:S(2)}) copy-start(f32[128]{0:T(128)S(1)} %broadcast_multiply_fusion.8) | copy-start | bytes 1540
  150.7 589.6 %copy-start.9 = (f32[128,1280]{1,0:T(8,128)}, f32[128,1280]{1,0:T(8,128)S(1)}, u32[]{:S(2)}) copy-start(f32[128,1280]{1,0:T(8,128)S(1)} %get-tuple-element.149) | copy-start | bytes 1966084
  151.0 106.5 %copy-start.71 = (f32[128]{0:T(128)}, f32[128]{0:T(128)S(1)}, u32[]{:S(2)}) copy-start(f32[128]{0:T(128)S(1)} %add_rsqrt_fusion) | copy-start | bytes 1540
  353.6 12.7 copy-start
  353.6 14.7 slice-start.4
  353.6 14.7 slice-start.5
  353.6 14.7 slice-start.6
  366.3 91.6 %copy-start.57 = (bf16[2,1,1280]{2,1,0:T(2,128)(2,1)}, bf16[2,1,1280]{2,1,0:T(2,128)(2,1)S(1)}, u32[]{:S(2)}) copy-start(bf16[2,1,1280]{2,1,0:T(2,128)(2,1)S(1)} %all-gather.2) | copy-start | bytes 15364
  370.8 93.7 %copy-start.45 = (bf16[128,1280]{1,0:T(8,128)(2,1)}, bf16[128,1280]{1,0:T(8,128)(2,1)S(1)}, u32[]{:S(2)}) copy-start(bf16[128,1280]{1,0:T(8,128)(2,1)S(1)} %fusion.26) | copy-start | bytes 983044
  375.1 216.5 %copy-start.59 = (bf16[2,1,1280]{2,1,0:T(2,128)(2,1)}, bf16[2,1,1280]{2,1,0:T(2,128)(2,1)S(1)}, u32[]{:S(2)}) copy-start(bf16[2,1,1280]{2,1,0:T(2,128)(2,1)S(1)} %all-gather.1) | copy-start | bytes 15364
  572.7 18.9 %slice-start = ((s8[13107200]{0:T(1024)(128)(4,1)}), s8[4194304]{0:T(1024)(128)(4,1)S(1)}, s32[]{:S(2)}) async-start(s8[13107200]{0:T(1024)(128)(4,1)} %bitcast.252), calls=%async_computation.20 | async-start | bytes 8388608
  572.7 18.9 %slice-start.1 = ((s8[13107200]{0:T(1024)(128)(4,1)}), s8[4194304]{0:T(1024)(128)(4,1)S(1)}, s32[]{:S(2)}) async-start(s8[13107200]{0:T(1024)(128)(4,1)} %bitcast.252), calls=%async_computation.21 | async-start | bytes 8388608
  579.0 12.7 slice-start.2
  579.0 12.7 slice-start.3
  615.8 12.7 copy-start.4
  662.4 249.4 %reduce-scatter.11.cloned.1.call-start = ((), (), s32[]{:S(2)}) async-start(), calls=%async_computation.13 | async-start | bytes 3481600 | tf_op jit(solution)/shard_map/reduce_scatter | solution.py:273
  707.8 44.0 %copy-start.21 = (f32[128,1280]{1,0:T(8,128)}, f32[128,1280]{1,0:T(8,128)S(1)}, u32[]{:S(2)}) copy-start(f32[128,1280]{1,0:T(8,128)S(1)} %scatter-add.9) | copy-start | bytes 1966084
  708.8 31.6 %copy-start.23 = (f32[128,1280]{1,0:T(8,128)}, f32[128,1280]{1,0:T(8,128)S(1)}, u32[]{:S(2)}) copy-start(f32[128,1280]{1,0:T(8,128)S(1)} %scatter-add.6) | copy-start | bytes 1966084
  720.0 10.6 copy-start.25
  720.0 10.6 copy-start.11
  730.6 9.8 copy-start.67
  730.6 9.8 copy-start.72
  740.4 10.4 copy-start.26
  740.4 10.4 copy-start.33
  755.7 231.0 %reduce-scatter.9.cloned.1.call-start = ((), (), s32[]{:S(2)}) async-start(), calls=%async_computation.12 | async-start | bytes 10444800 | tf_op jit(solution)/shard_map/reduce_scatter | solution.py:270
  785.3 9.1 copy-start.27
  786.1 8.4 copy-start.74
  786.1 8.4 copy-start.78
  805.6 14.4 copy-start.22
  805.6 323.3 %reduce-scatter.15.cloned.1.call-start = ((), (), s32[]{:S(2)}) async-start(), calls=%async_computation.15 | async-start | bytes 13926400 | tf_op jit(solution)/shard_map/reduce_scatter | solution.py:279
  835.7 14.5 copy-start.58
  835.8 435.3 %reduce-scatter.17.cloned.1.call-start = ((), (), s32[]{:S(2)}) async-start(), calls=%async_computation.16 | async-start | bytes 13926400 | tf_op jit(solution)/shard_map/reduce_scatter | solution.py:291
  868.0 14.0 copy-start.6
  868.0 544.5 %reduce-scatter.13.cloned.1.call-start = ((), (), s32[]{:S(2)}) async-start(), calls=%async_computation.14 | async-start | bytes 13926400 | tf_op jit(solution)/shard_map/reduce_scatter | solution.py:276
  900.8 592.8 %all-gather.23.cloned.1.call-start = ((), (), s32[]{:S(2)}) async-start(), calls=%async_computation.17 | async-start | bytes 2457600 | tf_op jit(solution)/shard_map/all_gather | solution.py:218
  901.6 631.7 %all-reduce.19.cloned.1.call-start = ((), (), s32[]{:S(2)}) async-start(), calls=%async_computation.19 | async-start | bytes 6553600 | tf_op jit(solution)/shard_map/psum | solution.py:305
  911.7 500.8 %copy-start.28 = (bf16[128,3,20,64]{0,3,2,1:T(8,128)(2,1)S(1)}, bf16[128,3,20,64]{0,3,2,1:T(8,128)(2,1)}, u32[]{:S(2)}) copy-start(bf16[128,3,20,64]{0,3,2,1:T(8,128)(2,1)} %copy-done.27) | copy-start | bytes 2949124
  1412.6 8.4 copy-start.65
  1412.6 8.4 copy-start.70
  1412.6 8.4 copy-start.55
  1412.6 8.4 copy-start.56
  1412.6 8.4 copy-start.53
  1412.6 8.4 copy-start.54
  1412.6 76.2 %copy-start.44 = (bf16[128,1280]{1,0:T(8,128)(2,1)S(1)}, bf16[128,1280]{1,0:T(8,128)(2,1)}, u32[]{:S(2)}) copy-start(bf16[128,1280]{1,0:T(8,128)(2,1)} %copy-done.43) | copy-start | bytes 983044
  1412.6 78.1 %copy-start.18 = (f32[128,1280]{1,0:T(8,128)S(1)}, f32[128,1280]{1,0:T(8,128)}, u32[]{:S(2)}) copy-start(f32[128,1280]{1,0:T(8,128)} %copy-done.17) | copy-start | bytes 1966084
  1412.7 78.1 %copy-start.20 = (f32[128,1280]{1,0:T(8,128)S(1)}, f32[128,1280]{1,0:T(8,128)}, u32[]{:S(2)}) copy-start(f32[128,1280]{1,0:T(8,128)} %copy-done.19) | copy-start | bytes 1966084
  (47 other events, 136.1 us)
Sparse Core Ops, SparseCore 0:
  10.4 87.1 all-gather.10
  99.9 44.1 all-gather.12
  146.4 102.8 all-gather.14
  251.4 102.1 all-gather.16
  355.7 102.1 all-gather.18
  460.1 102.1 all-gather.20
  662.5 136.5 reduce-scatter.18
  803.4 65.9 reduce-scatter.10
  873.5 113.2 reduce-scatter.8
  990.7 138.1 reduce-scatter.14
  1133.6 137.4 reduce-scatter.16
  1275.0 137.4 reduce-scatter.12
  1414.1 27.0 all-gather.22
  1443.8 89.4 all-reduce.18
